TPU v7x, 32 devices: a whole 2x2x4 slice. The times are simulated.
32 devices in a mesh: row: 16 (over z, x, core), col: 2 (over y).
Axes of the slice: x: 2, y: 2, z: 4, core: 2. Of those that a mesh axis runs over, the one named last changes fastest.
Arguments:
- x_train: bfloat16 [64, 8192], P(None, 'col'), may hold values from -8 to 8
- targets: float32 [8192], P('col'), may hold values from -6 to 6
- noise_draws: float32 [8192, 256], P('col', 'row'), may hold values from -3 to 3
- alpha_init: float32 [8192, 256], P('col', 'row'), may hold values from -6 to 6
- velocity_init: float32 [8192, 256], P('col', 'row'), may hold values from -3 to 3
- frequencies: bfloat16 [64, 4096], P(None, 'col'), may hold values from -5 to 5
- phases: float32 [4096], P('col'), may hold values from -3.140625 to 3.140625
- path_weights: bfloat16 [4096, 256], P('col'), may hold values from -6 to 6
- x_window: bfloat16 [64, 32768], P(None, 'row'), may hold values from -6 to 6
- batch_index: int32 [3, 8192], replicated, may hold values from 0 to 8191, as said below
Outputs:
- alpha_out: float32 [8192, 256], P('col', 'row')
- velocity_out: float32 [8192, 256], P('col', 'row')
- prior_window: float32 [256, 32768], P('col', 'row')
Inputs may be any that keep to these rules, and one draw needn't show every extreme that they name: `batch_index`: row b of every step names a training point of group g = (b // 256) % 2, that is a number from g * 4096 to (g + 1) * 4096 - 1; points may repeat.
All inputs are finite; a program needn't handle non-finite values.
Results may differ from a plain program's by a relative error of at most 0.0039.
Values may be sent and summed in bfloat16 or wider, within the bound.
A program may use at most 64 MiB of HBM per device.

v0:
```python
import functools

import jax
import jax.numpy as jnp
import numpy as np
from jax import lax
from jax.experimental import pallas as pl
from jax.experimental.pallas import tpu as pltpu
from jax.sharding import PartitionSpec as P

SQRT_THREE = 1.7320508075688772
LENGTH = 1.15
NOISE_VAR = 0.25
MOMENTUM = 0.9
STEP_SIZE = 0.5


def sine_coeffs(scale):
    nodes = 5
    k = np.arange(nodes)
    v = (np.cos((2 * k + 1) * np.pi / (2 * nodes)) + 1) / 2 / 16
    z = np.sqrt(v)
    q = np.sin(2 * np.pi * z) / z
    return [float(c * scale) for c in np.linalg.solve(np.vander(v, nodes, increasing=True), q)]


def scaled_cos(turns, coeffs):
    z = 0.25 - jnp.abs(turns - jnp.round(turns))
    v = z * z
    q = coeffs[-1]
    for c in coeffs[-2::-1]:
        q = q * v + c
    return q * z


def prior_kernel(coeffs, tile_f, freq_ref, phase_ref, weight_ref, point_ref, out_ref):
    feat = freq_ref.shape[0]
    points = point_ref[...]

    def body(i, acc):
        rows = pl.ds(pl.multiple_of(i * tile_f, tile_f), tile_f)
        arg = jnp.dot(freq_ref[rows, :], points, preferred_element_type=jnp.float32)
        turns = (arg + phase_ref[rows, :]) * (0.5 / np.pi)
        phi = scaled_cos(turns, coeffs).astype(jnp.bfloat16)
        return acc + lax.dot_general(
            weight_ref[rows, :], phi, (((0,), (0,)), ((), ())), preferred_element_type=jnp.float32
        )

    out_ref[...] = lax.fori_loop(0, feat // tile_f, body, jnp.zeros(out_ref.shape, jnp.float32))


def prior_sums(freq_t, phase_col, weights, points, total_feat):
    feat, d_in = freq_t.shape
    paths = weights.shape[1]
    n = points.shape[1]
    tile_n = min(512, n)
    coeffs = sine_coeffs((2.0 / total_feat) ** 0.5)
    return pl.pallas_call(
        functools.partial(prior_kernel, coeffs, min(256, feat)),
        grid=(n // tile_n,),
        in_specs=[
            pl.BlockSpec((feat, d_in), lambda i: (0, 0)),
            pl.BlockSpec((feat, 1), lambda i: (0, 0)),
            pl.BlockSpec((feat, paths), lambda i: (0, 0)),
            pl.BlockSpec((d_in, tile_n), lambda i: (0, i)),
        ],
        out_specs=pl.BlockSpec((paths, tile_n), lambda i: (0, i)),
        out_shape=jax.ShapeDtypeStruct((paths, n), jnp.float32),
        cost_estimate=pl.CostEstimate(
            flops=2 * feat * n * (paths + d_in), bytes_accessed=4 * paths * n, transcendentals=feat * n
        ),
    )(freq_t, phase_col, weights, points)


def matern(points, train):
    inner = lax.dot_general(
        train, points, (((0,), (0,)), ((), ())), preferred_element_type=jnp.float32
    )
    point_norm = jnp.sum(jnp.square(points.astype(jnp.float32)), axis=0)
    train_norm = jnp.sum(jnp.square(train.astype(jnp.float32)), axis=0)
    dist_sq = jnp.maximum(train_norm[:, None] + point_norm[None, :] - 2.0 * inner, 0.0)
    scaled = SQRT_THREE / LENGTH * jnp.sqrt(dist_sq)
    return ((1.0 + scaled) * jnp.exp(-scaled)).astype(jnp.bfloat16)


def point_counts(index, start, count):
    lanes = 128
    local = index - start
    high = (local // lanes)[:, None, :] == lax.broadcasted_iota(
        jnp.int32, (1, count // lanes, 1), 1
    )
    low = (local % lanes)[:, None, :] == lax.broadcasted_iota(jnp.int32, (1, lanes, 1), 1)
    tables = lax.dot_general(
        high.astype(jnp.bfloat16),
        low.astype(jnp.bfloat16),
        (((2,), (2,)), ((0,), (0,))),
        preferred_element_type=jnp.float32,
    )
    return tables.reshape(index.shape[0], count)


def shards(
    x_train,
    targets,
    noise_draws,
    alpha_init,
    velocity_init,
    frequencies,
    phases,
    path_weights,
    x_window,
    batch_index,
):
    row_count = lax.axis_size("row")
    col_count = lax.axis_size("col")
    row_id = lax.axis_index("row")
    col_id = lax.axis_index("col")
    train_cols = x_train.shape[1]
    own = train_cols // row_count
    steps = batch_index.shape[0]
    total_feat = frequencies.shape[1] * col_count

    mine = lax.dynamic_slice_in_dim(x_train, row_id * own, own, 1)
    points = lax.all_gather(mine, "col", axis=1, tiled=True)
    freq_t = frequencies.T
    phase_col = phases[:, None]
    kernel_tile = matern(points, x_train)
    prior_rows = prior_sums(freq_t, phase_col, path_weights, points, total_feat)
    window = prior_sums(freq_t, phase_col, path_weights, x_window, total_feat)
    prior_window = lax.psum_scatter(window, "col", scatter_dimension=0, tiled=True)

    counts = point_counts(batch_index, col_id * train_cols, train_cols)
    base = (noise_draws - targets[:, None]).T
    dual, velocity = alpha_init.T, velocity_init.T
    for step in range(steps):
        coeffs = lax.all_gather(dual.astype(jnp.bfloat16), "row", axis=0, tiled=True)
        sums = jnp.dot(coeffs, kernel_tile, preferred_element_type=jnp.float32) + prior_rows
        mine_sums = lax.psum_scatter(sums, "col", scatter_dimension=1, tiled=True)
        arrived = lax.all_to_all(mine_sums, "row", split_axis=0, concat_axis=1, tiled=True)
        gradient = counts[step][None, :] * (arrived + NOISE_VAR * dual + base)
        velocity = MOMENTUM * velocity - STEP_SIZE * gradient
        dual = dual + velocity
    return (dual.T, velocity.T, prior_window)


MESH = pl.DeviceIdType.MESH


def fused_kernel(
    scale_coeffs, steps, rows, x_ref, target_ref, noise_ref, alpha_in, velocity_in, freq_ref,
    phase_ref, weight_ref, window_ref, index_ref, alpha_ref, velocity_ref, prior_ref,
    count_ref, gathered, tile, train_prior, points, points_t, base, outboxes, arrivals, last_outbox, last_arrived,
    window_out, window_in,
    ring_send, ring_recv, pair_send, pair_recv, sum_send, sum_recv, misc_send, misc_recv,
):
    div, rem = lax.div, lax.rem
    row = lax.axis_index("row")
    col = lax.axis_index("col")
    peer = 1 - col
    devices = rows * 2
    flat = row * 2 + col
    paths = weight_ref.shape[0]
    share = paths // rows
    train = x_ref.shape[1]
    own = train // rows
    feat = freq_ref.shape[1]
    half = train // 2
    chips = rows // 2
    core = rem(row, 2)
    chip = div(row, 2)
    depth, side = div(chip, 2), rem(chip, 2)
    place = depth * (1 - side) + (chips - 1 - depth) * side

    def row_at(position, on_core):
        p = rem(position + 2 * chips, chips)
        back = div(p, chips // 2)
        return ((1 - back) * 2 * p + back * (2 * (chips - 1 - p) + 1)) * 2 + on_core

    def device(d):
        other = rem(flat + d, devices)
        return div(other, 2), rem(other, 2)

    barrier = pltpu.get_barrier_semaphore()

    def greet(d, carry):
        pl.semaphore_signal(barrier, inc=1, device_id=device(d), device_id_type=MESH)
        return carry

    lax.fori_loop(1, devices, greet, 0)

    def block(step, r, h):
        return gathered.at[
            step, pl.ds(pl.multiple_of(r * share, share), share), pl.ds(h * half, half)
        ]

    def whole_block(step, r):
        return gathered.at[step, pl.ds(pl.multiple_of(r * share, share), share), :]

    def ring_copy(step, way, k, h):
        sign = 1 - 2 * way
        ref = block(step, row_at(place - sign * k, core), h)
        return pltpu.make_async_remote_copy(
            src_ref=ref, dst_ref=ref,
            send_sem=ring_send.at[step, way, k, h], recv_sem=ring_recv.at[step, way, k, h],
            device_id=(row_at(place + sign, core), col), device_id_type=MESH,
        )

    def pair_copy(step, way, k, h):
        sign = 1 - 2 * way
        ref = block(step, row_at(place - sign * (k + 1), core), h)
        return pltpu.make_async_remote_copy(
            src_ref=ref, dst_ref=ref,
            send_sem=pair_send.at[step, way, k, h], recv_sem=pair_recv.at[step, way, k, h],
            device_id=(row + 1 - 2 * core, col), device_id_type=MESH,
        )

    def own_copy(step):
        ref = whole_block(step, row)
        return pltpu.make_async_remote_copy(
            src_ref=ref, dst_ref=ref,
            send_sem=misc_send.at[step], recv_sem=misc_recv.at[step],
            device_id=(row + 1 - 2 * core, col), device_id_type=MESH,
        )

    last = chips // 2 - 1

    def hops(action):
        def event(e, carry):
            k, h = div(e, 2), rem(e, 2)
            for way in (0, 1):
                @pl.when((k < last) | (h == way))
                def _():
                    action(way, k, h)
            return carry

        lax.fori_loop(0, 2 * (last + 1), event, 0)

    def gather(step, compute):
        gathered[step, pl.ds(pl.multiple_of(row * share, share), share), :] = alpha_ref[
            ...
        ].astype(jnp.bfloat16)
        for h in (0, 1):
            for way in (0, 1):
                ring_copy(step, way, 0, h).start()
        own_copy(step).start()

        def event(e, carry):
            compute(e)
            k, h = div(e, 2), rem(e, 2)
            for way in (0, 1):
                @pl.when((k < last) | (h == way))
                def _():
                    ring_copy(step, way, k, h).wait_recv()

                    @pl.when((k < last - 1) | ((k == last - 1) & (h == way)))
                    def _():
                        ring_copy(step, way, k + 1, h).start()

                    pair_copy(step, way, k, h).start()
            return carry

        lax.fori_loop(0, 2 * (last + 1), event, 0)
        own_copy(step).wait_recv()
        hops(lambda way, k, h: pair_copy(step, way, k, h).wait_recv())

    def boxes(step):
        if step < steps - 1:
            return outboxes.at[step], arrivals.at[step]
        return last_outbox, last_arrived

    def sum_copy(step, d):
        r, c = device(d)
        outbox, arrived = boxes(step)
        return pltpu.make_async_remote_copy(
            src_ref=outbox.at[
                pl.ds(pl.multiple_of(r * share, share), share),
                pl.ds(pl.multiple_of(c * own, own), own),
            ],
            dst_ref=arrived.at[col, :, pl.ds(pl.multiple_of(row * own, own), own)],
            send_sem=sum_send.at[step, d], recv_sem=sum_recv.at[step, d],
            device_id=(r, c), device_id_type=MESH,
        )

    def point_copy():
        return pltpu.make_async_remote_copy(
            src_ref=x_ref.at[:, pl.ds(pl.multiple_of(row * own, own), own)],
            dst_ref=points.at[col],
            send_sem=misc_send.at[steps], recv_sem=misc_recv.at[steps],
            device_id=(row, peer), device_id_type=MESH,
        )

    def window_copy(part):
        width = window_out.shape[2]
        return pltpu.make_async_remote_copy(
            src_ref=window_out.at[part], dst_ref=window_in.at[part],
            send_sem=misc_send.at[steps + 1 + part], recv_sem=misc_recv.at[steps + 1 + part],
            device_id=(row, peer), device_id_type=MESH,
        )

    alpha_ref[...] = alpha_in[...]
    velocity_ref[...] = velocity_in[...]
    base[...] = noise_ref[...] - target_ref[...]
    pl.semaphore_wait(barrier, devices - 1)
    point_copy().start()
    points[col] = x_ref[:, pl.ds(pl.multiple_of(row * own, own), own)]
    train_prior[...] = jnp.zeros_like(train_prior)
    events = 2 * (last + 1)

    def phi_block(pts_t, cols):
        arg = jnp.dot(pts_t, freq_ref[:, cols], preferred_element_type=jnp.float32)
        turns = (arg + phase_ref[:, cols]) * (0.5 / np.pi)
        return scaled_cos(turns, scale_coeffs).astype(jnp.bfloat16)

    def against(a, b):
        return lax.dot_general(
            a, b, (((1,), (1,)), ((), ())), preferred_element_type=jnp.float32
        )

    def train_work(e):
        @pl.when(e == 0)
        def _():
            point_copy().wait_recv()
            for c in (0, 1):
                points_t[c * own : (c + 1) * own, :] = points[c].astype(jnp.float32).T

        width = train // events
        cols = pl.ds(pl.multiple_of(e * width, width), width)
        trains = x_ref[:, cols]
        train_norm = jnp.sum(jnp.square(trains.astype(jnp.float32)), axis=0, keepdims=True)
        fwidth = feat // events
        fcols = pl.ds(pl.multiple_of(e * fwidth, fwidth), fwidth)
        group = 128

        def rows_of(i, carry):
            span = pl.ds(pl.multiple_of(i * group, group), group)
            pts = points_t[span, :]
            pts_norm = jnp.sum(jnp.square(pts), axis=1, keepdims=True)
            pts = pts.astype(jnp.bfloat16)
            inner = jnp.dot(pts, trains, preferred_element_type=jnp.float32)
            dist_sq = jnp.maximum(pts_norm + train_norm - 2.0 * inner, 0.0)
            scaled = SQRT_THREE / LENGTH * jnp.sqrt(dist_sq)
            tile[span, cols] = ((1.0 + scaled) * jnp.exp(-scaled)).astype(jnp.bfloat16)
            train_prior[:, span] += against(weight_ref[:, fcols], phi_block(pts, fcols))
            return carry

        lax.fori_loop(0, 2 * own // group, rows_of, 0)

    def count_points(step):
        lanes = 128
        local = index_ref[step : step + 1, :] - col * train
        high_ids = lax.broadcasted_iota(jnp.int32, (train // lanes, 1), 0)
        low_ids = lax.broadcasted_iota(jnp.int32, (lanes, 1), 0)
        high = ((local >> 7) == high_ids).astype(jnp.float32).astype(jnp.bfloat16)
        low = ((local & 127) == low_ids).astype(jnp.float32).astype(jnp.bfloat16)
        table = against(high, low)
        for i in range(train // lanes):
            count_ref[step : step + 1, i * lanes : (i + 1) * lanes] = table[i : i + 1, :]

    tiles = 2 * events
    wide = window_ref.shape[1] // tiles

    def window_work(part):
        def work(e):
            span = pl.ds(pl.multiple_of((part * events + e) * wide, wide), wide)
            pts = window_ref[:, span].astype(jnp.float32).T.astype(jnp.bfloat16)
            fwidth = min(512, feat)

            def feats(i, acc):
                fcols = pl.ds(pl.multiple_of(i * fwidth, fwidth), fwidth)
                return acc + against(weight_ref[:, fcols], phi_block(pts, fcols))

            acc = lax.fori_loop(
                0, feat // fwidth, feats, jnp.zeros((paths, wide), jnp.float32)
            )
            kept = paths // 2
            mine = jnp.where(col == 0, acc[:kept], acc[kept:])
            sent = jnp.where(col == 0, acc[kept:], acc[:kept])
            prior_ref[:, span] = mine
            window_out[part, :, pl.ds(pl.multiple_of(e * wide, wide), wide)] = sent.astype(
                jnp.bfloat16
            )

        return work

    for step in range(steps):
        if step == 0:
            gather(step, train_work)
        elif step < 3:
            gather(step, window_work(step - 1))
            window_copy(step - 1).start()
        else:
            gather(step, lambda e: None)
        outbox, arrived = boxes(step)
        for c in (0, 1):
            span = slice(c * own, (c + 1) * own)
            sums = against(gathered[step], tile[span, :]) + train_prior[:, span]
            outbox[:, span] = sums.astype(outbox.dtype)

        def send(d, carry):
            sum_copy(step, d).start()
            return carry

        lax.fori_loop(1, devices, send, 0)
        arrived[col, :, pl.ds(pl.multiple_of(row * own, own), own)] = outbox[
            pl.ds(pl.multiple_of(row * share, share), share),
            pl.ds(pl.multiple_of(col * own, own), own),
        ]

        count_points(step)

        def receive(d, carry):
            sum_copy(step, d).wait_recv()
            return carry

        lax.fori_loop(1, devices, receive, 0)
        total = arrived[0].astype(jnp.float32) + arrived[1].astype(jnp.float32)
        alpha = alpha_ref[...]
        gradient = count_ref[step : step + 1, :] * (total + NOISE_VAR * alpha + base[...])
        speed = MOMENTUM * velocity_ref[...] - STEP_SIZE * gradient
        velocity_ref[...] = speed
        alpha_ref[...] = alpha + speed

    for part in (0, 1):
        window_copy(part).wait()
        width = window_out.shape[2]
        span = slice(part * width, (part + 1) * width)
        prior_ref[:, span] = prior_ref[:, span] + window_in[part].astype(jnp.float32)
    point_copy().wait_send()
    for step in range(steps):
        own_copy(step).wait_send()
        hops(lambda way, k, h: ring_copy(step, way, k, h).wait_send())
        hops(lambda way, k, h: pair_copy(step, way, k, h).wait_send())

        def drain(d, carry):
            sum_copy(step, d).wait_send()
            return carry

        lax.fori_loop(1, devices, drain, 0)


def fused_shards(
    x_train, targets, noise_draws, alpha_init, velocity_init, frequencies, phases, path_weights,
    x_window, batch_index,
):
    rows = lax.axis_size("row")
    col_count = lax.axis_size("col")
    train = x_train.shape[1]
    steps = batch_index.shape[0]
    paths = path_weights.shape[1]
    share = paths // rows
    own = train // rows
    window = x_window.shape[1]
    coeffs = sine_coeffs((2.0 / (frequencies.shape[1] * col_count)) ** 0.5)
    vmem = pl.BlockSpec(memory_space=pltpu.VMEM)
    dma = pltpu.SemaphoreType.DMA
    hop_shape = (steps, 2, rows // 4, 2)
    alpha, velocity, prior = pl.pallas_call(
        functools.partial(fused_kernel, coeffs, steps, rows),
        in_specs=[vmem] * 10,
        out_specs=[vmem] * 3,
        out_shape=(
            jax.ShapeDtypeStruct((share, train), jnp.float32),
            jax.ShapeDtypeStruct((share, train), jnp.float32),
            jax.ShapeDtypeStruct((paths // 2, window), jnp.float32),
        ),
        scratch_shapes=[
            pltpu.VMEM((steps, train), jnp.float32),
            pltpu.VMEM((steps, paths, train), jnp.bfloat16),
            pltpu.VMEM((2 * own, train), jnp.bfloat16),
            pltpu.VMEM((paths, 2 * own), jnp.float32),
            pltpu.VMEM((2, x_train.shape[0], own), jnp.bfloat16),
            pltpu.VMEM((2 * own, x_train.shape[0]), jnp.float32),
            pltpu.VMEM((share, train), jnp.float32),
            pltpu.VMEM((steps - 1, paths, 2 * own), jnp.float32),
            pltpu.VMEM((steps - 1, 2, share, train), jnp.float32),
            pltpu.VMEM((paths, 2 * own), jnp.bfloat16),
            pltpu.VMEM((2, share, train), jnp.bfloat16),
            pltpu.VMEM((2, paths // 2, window // 2), jnp.bfloat16),
            pltpu.VMEM((2, paths // 2, window // 2), jnp.bfloat16),
            dma(hop_shape), dma(hop_shape), dma(hop_shape), dma(hop_shape),
            dma((steps, 2 * rows)), dma((steps, 2 * rows)),
            dma((steps + 3,)), dma((steps + 3,)),
        ],
        compiler_params=pltpu.CompilerParams(
            collective_id=0, has_side_effects=True, vmem_limit_bytes=48 * 1024 * 1024
        ),
    )(
        x_train, targets[None, :], noise_draws.T, alpha_init.T, velocity_init.T, frequencies,
        phases[None, :], path_weights.T, x_window, batch_index,
    )
    return alpha.T, velocity.T, prior


def solution(mesh):
    def body(*args):
        share = args[7].shape[1] // mesh.shape["row"]
        fits = share % 16 == 0 and mesh.shape["col"] == 2 and mesh.shape["row"] % 4 == 0
        return (fused_shards if fits and args[9].shape[0] >= 3 else shards)(*args)

    placed = (
        P(None, "col"),
        P("col"),
        P("col", "row"),
        P("col", "row"),
        P("col", "row"),
        P(None, "col"),
        P("col"),
        P("col", None),
        P(None, "row"),
        P(),
    )
    return jax.shard_map(
        body,
        mesh=mesh,
        in_specs=placed,
        out_specs=(P("col", "row"), P("col", "row"), P("col", "row")),
        check_vma=False,
    )
```

profile of v0, /device:TPU:0, one launch (start us, length us, event | category | flops | bytes accessed | tf_op | source)
XLA Modules:
  0.0 115.4 jit_solution(12005054185972532806)
XLA Ops:
  0.6 0.0 copy-start
  0.6 0.0 copy-start.1
  0.7 0.0 copy-start.2
  0.7 0.0 copy-start.3
  0.7 0.0 copy-start.4
  0.7 0.0 copy-start.5
  0.7 0.0 copy-start.6
  0.7 0.0 copy-start.7
  0.7 0.0 copy-start.8
  0.7 1.6 %copy.13 = bf16[2048,256]{0,1:T(8,128)(2,1)S(1)} copy(bf16[2048,256]{1,0:T(8,128)(2,1)} %param.17) | data formatting | bytes 2097152 | tf_op args[7]
  2.3 0.0 copy-done
  2.4 0.0 copy-done.1
  2.4 0.0 copy-done.2
  2.4 0.0 copy-done.3
  2.4 0.0 copy-done.4
  2.4 0.0 copy-done.5
  2.4 0.0 copy-done.6
  2.4 0.0 copy-done.7
  2.4 0.0 copy-done.8
  2.4 110.6 %shard_map.121 = (f32[16,4096]{1,0:T(8,128)S(1)}, f32[16,4096]{1,0:T(8,128)S(1)}, f32[128,2048]{1,0:T(8,128)S(1)}) custom-call(bf16[64,4096]{1,0:T(8,128)(2,1)S(1)} %copy-done, f32[1,4096]{1,0:T(1,128)S(1)} %bitcast.14, f32[16,4096]{1,0:T(8,128)S(1)} %bitcast.9, f32[16,4096]{1,0:T(8,128)S(1)} %bitcast.10, f32[16,4096]{1,0:T(8,128)S(1)} %bitcast.11, ...), custom_call_target="tpu_custom_call" | custom-call | tf_op jit(solution)/shard_map/pallas_call | solution.py:457
  113.0 0.7 copy.17
  113.7 0.7 copy.18
  114.5 1.0 copy.19
Async XLA Ops:
  0.6 1.7 %copy-start = (bf16[64,4096]{1,0:T(8,128)(2,1)S(1)}, bf16[64,4096]{1,0:T(8,128)(2,1)}, u32[]{:S(2)}) copy-start(bf16[64,4096]{1,0:T(8,128)(2,1)} %x_ref.1) | copy-start | bytes 1572868
  0.6 1.7 %copy-start.1 = (f32[4096,16]{0,1:T(8,128)S(1)}, f32[4096,16]{0,1:T(8,128)}, u32[]{:S(2)}) copy-start(f32[4096,16]{0,1:T(8,128)} %param.12) | copy-start | bytes 786436
  0.7 1.7 %copy-start.2 = (f32[4096,16]{0,1:T(8,128)S(1)}, f32[4096,16]{0,1:T(8,128)}, u32[]{:S(2)}) copy-start(f32[4096,16]{0,1:T(8,128)} %param.13) | copy-start | bytes 786436
  0.7 1.7 %copy-start.3 = (f32[4096,16]{0,1:T(8,128)S(1)}, f32[4096,16]{0,1:T(8,128)}, u32[]{:S(2)}) copy-start(f32[4096,16]{0,1:T(8,128)} %param.14) | copy-start | bytes 786436
  0.7 1.7 %copy-start.4 = (bf16[64,2048]{1,0:T(8,128)(2,1)S(1)}, bf16[64,2048]{1,0:T(8,128)(2,1)}, u32[]{:S(2)}) copy-start(bf16[64,2048]{1,0:T(8,128)(2,1)} %freq_ref.1) | copy-start | bytes 786436
  0.7 1.7 %copy-start.5 = (bf16[64,2048]{1,0:T(8,128)(2,1)S(1)}, bf16[64,2048]{1,0:T(8,128)(2,1)}, u32[]{:S(2)}) copy-start(bf16[64,2048]{1,0:T(8,128)(2,1)} %window_ref.1) | copy-start | bytes 786436
  0.7 1.7 %copy-start.6 = (s32[3,8192]{1,0:T(4,128)S(1)}, s32[3,8192]{1,0:T(4,128)}, u32[]{:S(2)}) copy-start(s32[3,8192]{1,0:T(4,128)} %index_ref.1) | copy-start | bytes 294916
  0.7 1.7 %copy-start.7 = (f32[4096]{0:T(1024)S(1)}, f32[4096]{0:T(1024)}, u32[]{:S(2)}) copy-start(f32[4096]{0:T(1024)} %param.11) | copy-start | bytes 49156
  0.7 1.7 %copy-start.8 = (f32[2048]{0:T(1024)S(1)}, f32[2048]{0:T(1024)}, u32[]{:S(2)}) copy-start(f32[2048]{0:T(1024)} %param.16) | copy-start | bytes 24580
where the time goes:
time: 116 us; the launch traced here: 115 us
  Pallas kernels  111 us (96%)
  local copies, waits for them, and re-layouts  4.03 us (3%)
    pallas_call x1, Pallas kernels, fused_shards(): pl.pallas_call(functools.partial(fused_kernel, coeffs, steps, rows), in_s...  111 us
    unnamed x22, local copies, waits for them, and re-layouts  4.03 us

commit v1 on v0

v1 whole, which is shorter than its diff:
```python
import functools

import jax
import jax.numpy as jnp
import numpy as np
from jax import lax
from jax.experimental import pallas as pl
from jax.experimental.pallas import tpu as pltpu
from jax.sharding import PartitionSpec as P

SQRT_THREE = 1.7320508075688772
LENGTH = 1.15
NOISE_VAR = 0.25
MOMENTUM = 0.9
STEP_SIZE = 0.5


def sine_coeffs(scale):
    nodes = 4
    k = np.arange(nodes)
    v = (np.cos((2 * k + 1) * np.pi / (2 * nodes)) + 1) / 2 / 16
    z = np.sqrt(v)
    q = np.sin(2 * np.pi * z) / z
    return [float(c * scale) for c in np.linalg.solve(np.vander(v, nodes, increasing=True), q)]


def scaled_cos(turns, coeffs):
    z = 0.25 - jnp.abs(turns - jnp.round(turns))
    v = z * z
    q = coeffs[-1]
    for c in coeffs[-2::-1]:
        q = q * v + c
    return q * z


def prior_kernel(coeffs, tile_f, freq_ref, phase_ref, weight_ref, point_ref, out_ref):
    feat = freq_ref.shape[0]
    points = point_ref[...]

    def body(i, acc):
        rows = pl.ds(pl.multiple_of(i * tile_f, tile_f), tile_f)
        arg = jnp.dot(freq_ref[rows, :], points, preferred_element_type=jnp.float32)
        turns = (arg + phase_ref[rows, :]) * (0.5 / np.pi)
        phi = scaled_cos(turns, coeffs).astype(jnp.bfloat16)
        return acc + lax.dot_general(
            weight_ref[rows, :], phi, (((0,), (0,)), ((), ())), preferred_element_type=jnp.float32
        )

    out_ref[...] = lax.fori_loop(0, feat // tile_f, body, jnp.zeros(out_ref.shape, jnp.float32))


def prior_sums(freq_t, phase_col, weights, points, total_feat):
    feat, d_in = freq_t.shape
    paths = weights.shape[1]
    n = points.shape[1]
    tile_n = min(512, n)
    coeffs = sine_coeffs((2.0 / total_feat) ** 0.5)
    return pl.pallas_call(
        functools.partial(prior_kernel, coeffs, min(256, feat)),
        grid=(n // tile_n,),
        in_specs=[
            pl.BlockSpec((feat, d_in), lambda i: (0, 0)),
            pl.BlockSpec((feat, 1), lambda i: (0, 0)),
            pl.BlockSpec((feat, paths), lambda i: (0, 0)),
            pl.BlockSpec((d_in, tile_n), lambda i: (0, i)),
        ],
        out_specs=pl.BlockSpec((paths, tile_n), lambda i: (0, i)),
        out_shape=jax.ShapeDtypeStruct((paths, n), jnp.float32),
        cost_estimate=pl.CostEstimate(
            flops=2 * feat * n * (paths + d_in), bytes_accessed=4 * paths * n, transcendentals=feat * n
        ),
    )(freq_t, phase_col, weights, points)


def matern(points, train):
    inner = lax.dot_general(
        train, points, (((0,), (0,)), ((), ())), preferred_element_type=jnp.float32
    )
    point_norm = jnp.sum(jnp.square(points.astype(jnp.float32)), axis=0)
    train_norm = jnp.sum(jnp.square(train.astype(jnp.float32)), axis=0)
    dist_sq = jnp.maximum(train_norm[:, None] + point_norm[None, :] - 2.0 * inner, 0.0)
    scaled = SQRT_THREE / LENGTH * jnp.sqrt(dist_sq)
    return ((1.0 + scaled) * jnp.exp(-scaled)).astype(jnp.bfloat16)


def point_counts(index, start, count):
    lanes = 128
    local = index - start
    high = (local // lanes)[:, None, :] == lax.broadcasted_iota(
        jnp.int32, (1, count // lanes, 1), 1
    )
    low = (local % lanes)[:, None, :] == lax.broadcasted_iota(jnp.int32, (1, lanes, 1), 1)
    tables = lax.dot_general(
        high.astype(jnp.bfloat16),
        low.astype(jnp.bfloat16),
        (((2,), (2,)), ((0,), (0,))),
        preferred_element_type=jnp.float32,
    )
    return tables.reshape(index.shape[0], count)


def shards(
    x_train,
    targets,
    noise_draws,
    alpha_init,
    velocity_init,
    frequencies,
    phases,
    path_weights,
    x_window,
    batch_index,
):
    row_count = lax.axis_size("row")
    col_count = lax.axis_size("col")
    row_id = lax.axis_index("row")
    col_id = lax.axis_index("col")
    train_cols = x_train.shape[1]
    own = train_cols // row_count
    steps = batch_index.shape[0]
    total_feat = frequencies.shape[1] * col_count

    mine = lax.dynamic_slice_in_dim(x_train, row_id * own, own, 1)
    points = lax.all_gather(mine, "col", axis=1, tiled=True)
    freq_t = frequencies.T
    phase_col = phases[:, None]
    kernel_tile = matern(points, x_train)
    prior_rows = prior_sums(freq_t, phase_col, path_weights, points, total_feat)
    window = prior_sums(freq_t, phase_col, path_weights, x_window, total_feat)
    prior_window = lax.psum_scatter(window, "col", scatter_dimension=0, tiled=True)

    counts = point_counts(batch_index, col_id * train_cols, train_cols)
    base = (noise_draws - targets[:, None]).T
    dual, velocity = alpha_init.T, velocity_init.T
    for step in range(steps):
        coeffs = lax.all_gather(dual.astype(jnp.bfloat16), "row", axis=0, tiled=True)
        sums = jnp.dot(coeffs, kernel_tile, preferred_element_type=jnp.float32) + prior_rows
        mine_sums = lax.psum_scatter(sums, "col", scatter_dimension=1, tiled=True)
        arrived = lax.all_to_all(mine_sums, "row", split_axis=0, concat_axis=1, tiled=True)
        gradient = counts[step][None, :] * (arrived + NOISE_VAR * dual + base)
        velocity = MOMENTUM * velocity - STEP_SIZE * gradient
        dual = dual + velocity
    return (dual.T, velocity.T, prior_window)


MESH = pl.DeviceIdType.MESH
TURN = 1.0 / (2.0 * np.pi)
DIST_SCALE = 3.0 / (LENGTH * LENGTH)


def split_three(value):
    parts = []
    for _ in range(3):
        part = value.astype(jnp.bfloat16).astype(jnp.float32)
        parts.append(part)
        value = value - part
    return parts


def tail_rows(rows, count, n):
    at = lax.broadcasted_iota(jnp.int32, (count, n), 0)
    tail = jnp.zeros((count, n), jnp.float32)
    for i, row in enumerate(rows):
        tail = jnp.where(at == i, row, tail)
    return tail


DIMS = "yxz"
LOADS = (
    "alpha", "x", "index", "target", "noise", "velocity", "freq", "phase", "weight", "window",
)
PIECES = ((0, 256, "yxz"), (256, 256, "yzx"))
MASKS = ("y", "x", "z", "yx", "yz", "xz", "yxz")


def mask_of(dims):
    return "".join(d for d in DIMS if d in dims)


def fused_kernel(
    scale_coeffs, steps, rows, pieces, x_hbm, target_hbm, noise_hbm, alpha_hbm, velocity_hbm,
    freq_hbm, phase_hbm, weight_hbm, window_hbm, index_hbm, alpha_ref, velocity_ref, prior_ref,
    x_ref, target_ref, noise_ref, alpha_in, velocity_in, freq_ref, phase_ref, weight_ref,
    window_ref, index_ref, load_sem,
    gathered, tile, train_aug, window_aug, point_aug, freq_t, weight_t, phi_buf, acc,
    pull_a, pull_v, prior_t, prior_out, prior_in, count_ref, count_t, x_in, start_out, start_in, entry_out, entry_in,
    exit_out, exit_in, window_acc, window_out, window_in,
    hop_send, hop_recv, pair_send, pair_recv, entry_send, entry_recv, exit_send, exit_recv,
    misc_send, misc_recv,
):
    div, rem = lax.div, lax.rem
    f32, bf16 = jnp.float32, jnp.bfloat16
    row = lax.axis_index("row")
    col = lax.axis_index("col")
    peer = 1 - col
    devices = rows * 2
    paths = weight_ref.shape[1]
    share = paths // rows
    kept = paths // 2
    train = x_ref.shape[1]
    team = rows // 2
    own = train // team
    feat = freq_ref.shape[1]
    d_in = x_ref.shape[0]
    window = window_ref.shape[1]
    core = rem(row, 2)
    group = div(row, team)
    local = rem(row, team)
    flip = {"x": 2 - 4 * rem(div(row, 2), 2), "z": 4 - 8 * rem(div(row, 4), 2)}
    sibling = row + 1 - 2 * core
    block = 256

    def at(start, size, unit=None):
        return pl.ds(pl.multiple_of(start, unit or size), size)

    def mate(d):
        return rem(local + d + 1, team)

    def remote(src, dst, send, recv, device):
        return pltpu.make_async_remote_copy(
            src_ref=src, dst_ref=dst, send_sem=send, recv_sem=recv,
            device_id=device, device_id_type=MESH,
        )

    def loop(n, action):
        def one(i, carry):
            action(i)
            return carry

        lax.fori_loop(0, n, one, 0)

    def load(name):
        i = LOADS.index(name)
        src, dst = (
            (alpha_hbm, alpha_in), (x_hbm, x_ref), (index_hbm, index_ref),
            (target_hbm, target_ref), (noise_hbm, noise_ref), (velocity_hbm, velocity_in),
            (freq_hbm, freq_ref), (phase_hbm, phase_ref), (weight_hbm, weight_ref),
            (window_hbm, window_ref),
        )[i]
        return pltpu.make_async_copy(src, dst, load_sem.at[i])

    def loaded(*names):
        for name in names:
            load(name).wait()

    barrier = pltpu.get_barrier_semaphore()
    pl.semaphore_signal(barrier, inc=1, device_id=(row, peer), device_id_type=MESH)
    loop(team - 1, lambda d: pl.semaphore_signal(
        barrier, inc=1, device_id=(group * team + mate(d), col), device_id_type=MESH
    ))
    for name in LOADS:
        load(name).start()

    def source(mask):
        r = row
        for d in "xz":
            r = r + flip[d] if d in mask else r
        return r, (peer if "y" in mask else col)

    def first_row(r, c):
        return (c * team + rem(r, team)) * own

    def piece(step, mask, q, twin=False):
        r, c = source(mask)
        r = r + 1 - 2 * core if twin else r
        start, size, _ = pieces[q]
        return gathered.at[step, at(first_row(r, c) + start, size, 16), :]

    def hop(step, mask, d, q):
        ref = piece(step, mask, q)
        i = MASKS.index(mask_of(mask + d))
        return remote(
            ref, ref, hop_send.at[step, q, i], hop_recv.at[step, q, i], source(d)
        )

    def arrival(step, mask, q):
        ref = piece(step, mask, q)
        i = MASKS.index(mask)
        return remote(ref, ref, hop_send.at[step, q, i], hop_recv.at[step, q, i], (sibling, col))

    def pair(step, mask, q, twin=False):
        ref = piece(step, mask, q, twin)
        i = MASKS.index(mask) + 1 if mask else 0
        return remote(
            ref, ref, pair_send.at[step, q, i], pair_recv.at[step, q, i], (sibling, col)
        )

    count = range(len(pieces))

    def start_gather(step):
        for place in range(3):
            for q in count:
                hop(step, "", pieces[q][2][place], q).start()
        for q in count:
            pair(step, "", q).start()

    def relay(step, which):
        for q in count:
            order = pieces[q][2]
            mask = mask_of([order[i] for i in which])
            arrival(step, mask, q).wait_recv()
            for d in order[max(which) + 1 :]:
                hop(step, mask, d, q).start()
            pair(step, mask, q).start()

    def product(step, masks):
        for mask in masks:
            for q in count:
                pair(step, mask, q, True).wait_recv()
        wide = 2 * len(masks)
        r, c = source(masks[0])
        first = (c * team + div(rem(r, team), wide) * wide) * own
        span = at(first, wide * own)
        return dot(tile[:, span], gathered[step, span, :])

    def x_copy():
        half = train // 2
        cols = at(core * half, half)
        return remote(
            x_ref.at[:, cols], x_in.at[:, cols], misc_send.at[0], misc_recv.at[0], (row, peer)
        )

    def x_pair():
        half = train // 2
        ref = x_in.at[:, at(core * half, half)]
        return remote(ref, ref, misc_send.at[1], misc_recv.at[1], (sibling, col))

    def x_twin():
        half = train // 2
        ref = x_in.at[:, at((1 - core) * half, half)]
        return remote(ref, ref, misc_send.at[1], misc_recv.at[1], (sibling, col))

    def prior_copy():
        return remote(prior_out, prior_in, misc_send.at[2], misc_recv.at[2], (row, peer))

    parts = window_out.shape[0]

    def window_copy(part):
        return remote(
            window_out.at[part], window_in.at[part],
            misc_send.at[3 + part], misc_recv.at[3 + part], (row, peer),
        )

    def entry_refs(kind):
        if kind == 0:
            return start_out, start_in
        return entry_out.at[kind - 1], entry_in.at[kind - 1]

    def entry_copy(kind, d):
        m = mate(d)
        out, into = entry_refs(kind)
        return remote(
            out.at[:, at(m * own, own)], into.at[at(local * share, share), :],
            entry_send.at[kind, m], entry_recv.at[kind, local], (group * team + m, col),
        )

    def entry_arrival(kind, d):
        m = mate(d)
        out, into = entry_refs(kind)
        return remote(
            out.at[:, at(m * own, own)], into.at[at(m * share, share), :],
            entry_send.at[kind, m], entry_recv.at[kind, m], (group * team + m, col),
        )

    def send_entry(kind, value):
        out, into = entry_refs(kind)
        if kind:
            out[...] = value
        loop(team - 1, lambda d: entry_copy(kind, d).start())
        into[at(local * share, share), :] = out[:, at(local * own, own)]

    def take_entry(kind):
        loop(team - 1, lambda d: entry_arrival(kind, d).wait_recv())
        return entry_refs(kind)[1][...].astype(f32).T

    def exit_copy(kind, d):
        m = mate(d)
        return remote(
            exit_out.at[kind, at(m * share, share), :],
            exit_in.at[kind, :, at(local * own, own)],
            exit_send.at[kind, m], exit_recv.at[kind, local], (group * team + m, col),
        )

    def exit_arrival(kind, d):
        m = mate(d)
        return remote(
            exit_out.at[kind, at(m * share, share), :],
            exit_in.at[kind, :, at(m * own, own)],
            exit_send.at[kind, m], exit_recv.at[kind, m], (group * team + m, col),
        )

    def send_exit(kind, value):
        exit_out[kind] = value.T.astype(bf16)
        loop(team - 1, lambda d: exit_copy(kind, d).start())
        exit_in[kind, :, at(local * own, own)] = exit_out[kind, at(local * share, share), :]

    def take_exit(kind):
        loop(team - 1, lambda d: exit_arrival(kind, d).wait_recv())
        return exit_in[kind].astype(f32)

    def dot(a, b):
        return jnp.dot(a, b, preferred_element_type=f32)

    def against(a, b):
        return lax.dot_general(a, b, (((1,), (1,)), ((), ())), preferred_element_type=f32)

    def add_train(ref, c):
        def one(i):
            x = ref[:, at(i * block, block)]
            cols = at(c * train + i * block, block)
            for part in range(3):
                train_aug[part * d_in : (part + 1) * d_in, cols] = x
            norm = DIST_SCALE * jnp.sum(jnp.square(x.astype(f32)), axis=0, keepdims=True)
            tail = tail_rows([1.0, 1.0, 1.0] + split_three(norm), 16, block)
            train_aug[3 * d_in : 3 * d_in + 16, cols] = tail.astype(bf16)
            train_aug[3 * d_in + 16 :, cols] = jnp.zeros((d_in - 16, block), bf16)

        loop(train // block, one)

    def add_points():
        for i in range(own // block):
            x = x_ref[:, at(local * own + i * block, block)].astype(f32)
            norm = DIST_SCALE * jnp.sum(jnp.square(x), axis=0, keepdims=True)
            tail = tail_rows(split_three(norm) + [1.0, 1.0, 1.0], d_in, block)
            stack = jnp.concatenate(split_three(-2.0 * DIST_SCALE * x) + [tail], axis=0)
            point_aug[i * block : (i + 1) * block, :] = stack.T.astype(bf16)

    def add_window():
        for part in range(3):
            window_aug[part * d_in : (part + 1) * d_in, :] = window_ref[...]
        window_aug[3 * d_in :, :] = tail_rows([1.0] * 3, d_in, window).astype(bf16)

    def add_freq():
        def one(i):
            cols = at(i * block, block)
            tail = tail_rows(split_three(phase_ref[:, cols] * TURN), d_in, block)
            stack = jnp.concatenate(
                split_three(freq_ref[:, cols].astype(f32) * TURN) + [tail], axis=0
            )
            freq_t[cols, :] = stack.T.astype(bf16)
            weight_t[:, cols] = weight_ref[cols, :].astype(f32).T.astype(bf16)

        loop(feat // block, one)

    def count_points(step):
        lanes = 128
        width = index_ref.shape[1] // devices
        index = jnp.concatenate(
            [index_ref[step : step + 1, at((2 * i + col) * width, width)] for i in range(rows)],
            axis=1,
        )
        index = index - col * train
        high_ids = lax.broadcasted_iota(jnp.int32, (train // lanes, 1), 0)
        low_ids = lax.broadcasted_iota(jnp.int32, (lanes, 1), 0)
        high = ((index >> 7) == high_ids).astype(f32).astype(bf16)
        low = ((index & 127) == low_ids).astype(f32).astype(bf16)
        table = against(high, low)
        for i in range(train // lanes):
            count_ref[step : step + 1, i * lanes : (i + 1) * lanes] = table[i : i + 1, :]

    def spread_counts():
        for step in range(steps):
            line = count_ref[step : step + 1, at(local * own, own)]
            count_t[step] = jnp.broadcast_to(line, (kept, own)).T

    def fill_phi(rhs, first, n):
        width = 512

        def one(i):
            turns = dot(freq_t[at(first + i * width, width), :], rhs)
            phi_buf[at(i * width, width), :] = scaled_cos(turns, scale_coeffs).astype(bf16)

        loop(n // width, one)

    def prior_points(c, out):
        def one(i):
            fill_phi(train_aug[:, at(c * train + local * own + i * block, block)], 0, feat)
            out[at(i * block, block), :] = dot(weight_t[at(group * kept, kept), :], phi_buf[...]).T

        loop(own // block, one)

    def fill_tile(i):
        cols = at(i * block, block)
        dist_sq = jnp.maximum(dot(point_aug[...], train_aug[:, cols]), 1e-30)
        scaled = dist_sq * lax.rsqrt(dist_sq)
        tile[:, cols] = ((1.0 + scaled) * jnp.exp(-scaled)).astype(bf16)

    tiles = train // block

    def fill_tiles(c, first, n):
        loop(n, lambda i: fill_tile(c * tiles + first + i))

    def window_work(i, f):
        half = feat // 2
        span = at(i * block, block)
        fill_phi(window_aug[:, span], f * half, half)
        sums = dot(weight_t[:, at(f * half, half)], phi_buf[:half, :])
        if f == 0:
            window_acc[...] = sums
            return
        total = window_acc[...] + sums
        prior_ref[:, span] = jnp.where(col == 0, total[:kept], total[kept:])
        per = window // block // parts
        window_out[i // per, :, (i % per) * block : (i % per + 1) * block] = jnp.where(
            col == 0, total[kept:], total[:kept]
        ).astype(bf16)
        if i % per == per - 1:
            window_copy(i // per).start()

    loaded("alpha")
    start_out[...] = alpha_in[...].astype(bf16)
    pl.semaphore_wait(barrier, team)
    send_entry(0, None)
    loaded("x")
    x_copy().start()
    loaded("index")
    for step in range(steps):
        count_points(step)
    loaded("target", "noise", "velocity")
    base = noise_ref[...] - target_ref[...]
    speed = velocity_in[...]
    free = alpha_in[...]
    for step in range(steps):
        speed = MOMENTUM * speed - STEP_SIZE * (
            count_ref[step : step + 1, :] * (NOISE_VAR * free + base)
        )
        if step < steps - 1:
            free = free + speed
            send_entry(1 + step, free)
    alpha_ref[...] = free
    velocity_ref[...] = speed
    add_train(x_ref, col)
    add_points()
    fill_tiles(col, 0, 4)
    gathered[0, at(first_row(row, col), own), :] = take_entry(0).astype(bf16)
    start_gather(0)
    loaded("freq", "phase", "weight")
    add_freq()
    fill_tiles(col, 4, tiles - 4)
    relay(0, (0,))
    relay(0, (1,))
    relay(0, (2,))
    x_copy().wait_recv()
    x_pair().start()
    prior_points(col, prior_t)
    relay(0, (0, 1))
    x_twin().wait_recv()
    add_train(x_in, peer)
    prior_points(peer, prior_out)
    prior_copy().start()
    relay(0, (0, 2))
    relay(0, (1, 2))
    fill_tiles(peer, 0, tiles // 2)
    relay(0, (0, 1, 2))
    fill_tiles(peer, tiles // 2, tiles // 2)
    spread_counts()
    loaded("window")
    add_window()
    for mask in ("",) + MASKS:
        for q in count:
            pair(0, mask, q, True).wait_recv()
    acc[...] = dot(tile[...], gathered[0])
    prior_copy().wait_recv()
    prior_t[...] += prior_in[...]

    for step in range(1, steps + 1):
        sums = acc[...] + prior_t[...]
        if step == 1:
            speed = -STEP_SIZE * (count_t[0] * sums)
            pull = speed
        else:
            pull = pull_a[...]
            speed = MOMENTUM * pull_v[...] - STEP_SIZE * (
                count_t[step - 1] * (sums + NOISE_VAR * pull)
            )
            pull = pull + speed
        if step == steps:
            send_exit(1, speed)
            break
        pull_v[...] = speed
        pull_a[...] = pull
        gathered[step, at(first_row(row, col), own), :] = (take_entry(step) + pull).astype(bf16)
        start_gather(step)
        chunks = window // block // (steps - 1)
        work = [
            (lambda i, f: lambda: window_work(i, f))((step - 1) * chunks + i, f)
            for i in range(chunks) for f in (0, 1)
        ]

        def run(n):
            for _ in range(n):
                work.pop(0)()

        run(3)
        relay(step, (0,))
        relay(step, (1,))
        relay(step, (2,))
        run(2)
        relay(step, (0, 1))
        acc[...] = product(step, ("", "x"))
        run(1)
        relay(step, (0, 2))
        relay(step, (1, 2))
        if step == steps - 1:
            send_exit(0, pull_a[...])
        run(len(work))
        acc[...] += product(step, ("y", "yx"))
        relay(step, (0, 1, 2))
        acc[...] += product(step, ("z", "xz"))
        acc[...] += product(step, ("yz",))
        acc[...] += product(step, ("yxz",))

    alpha_ref[...] += take_exit(0)
    for part in range(parts):
        window_copy(part).wait()
        width = window // parts
        span = slice(part * width, (part + 1) * width)
        prior_ref[:, span] = prior_ref[:, span] + window_in[part].astype(f32)
    speed = velocity_ref[...] + take_exit(1)
    velocity_ref[...] = speed
    alpha_ref[...] += speed
    x_copy().wait_send()
    x_pair().wait_send()
    prior_copy().wait_send()
    for kind in range(steps):
        loop(team - 1, lambda d: entry_copy(kind, d).wait_send())
    for kind in range(2):
        loop(team - 1, lambda d: exit_copy(kind, d).wait_send())
    for step in range(steps):
        for q in count:
            for mask in MASKS:
                arrival(step, mask, q).wait_send()
                pair(step, mask, q).wait_send()
            pair(step, "", q).wait_send()


def fused_shards(
    x_train, targets, noise_draws, alpha_init, velocity_init, frequencies, phases, path_weights,
    x_window, batch_index,
):
    rows = lax.axis_size("row")
    col_count = lax.axis_size("col")
    d_in, train = x_train.shape
    steps = batch_index.shape[0]
    feat, paths = path_weights.shape
    share = paths // rows
    own = 2 * train // rows
    kept = paths // 2
    window = x_window.shape[1]
    parts = 4
    coeffs = sine_coeffs((2.0 / (feat * col_count)) ** 0.5)
    vmem = pl.BlockSpec(memory_space=pltpu.VMEM)
    dma = pltpu.SemaphoreType.DMA
    f32, bf16 = jnp.float32, jnp.bfloat16
    n = len(PIECES)
    alpha, velocity, prior = pl.pallas_call(
        functools.partial(fused_kernel, coeffs, steps, rows, PIECES),
        in_specs=[pl.BlockSpec(memory_space=pltpu.HBM)] * 10,
        out_specs=[vmem] * 3,
        out_shape=(
            jax.ShapeDtypeStruct((share, train), f32),
            jax.ShapeDtypeStruct((share, train), f32),
            jax.ShapeDtypeStruct((kept, window), f32),
        ),
        scratch_shapes=[
            pltpu.VMEM((d_in, train), bf16),
            pltpu.VMEM((1, train), f32),
            pltpu.VMEM((share, train), f32),
            pltpu.VMEM((share, train), f32),
            pltpu.VMEM((share, train), f32),
            pltpu.VMEM((d_in, feat), bf16),
            pltpu.VMEM((1, feat), f32),
            pltpu.VMEM((feat, paths), bf16),
            pltpu.VMEM((d_in, window), bf16),
            pltpu.VMEM(batch_index.shape, jnp.int32),
            dma((10,)),
            pltpu.VMEM((steps, 2 * train, kept), bf16),
            pltpu.VMEM((own, 2 * train), bf16),
            pltpu.VMEM((4 * d_in, 2 * train), bf16),
            pltpu.VMEM((4 * d_in, window), bf16),
            pltpu.VMEM((own, 4 * d_in), bf16),
            pltpu.VMEM((feat, 4 * d_in), bf16),
            pltpu.VMEM((paths, feat), bf16),
            pltpu.VMEM((feat, 256), bf16),
            pltpu.VMEM((own, kept), f32),
            pltpu.VMEM((own, kept), f32),
            pltpu.VMEM((own, kept), f32),
            pltpu.VMEM((own, kept), f32),
            pltpu.VMEM((own, kept), f32),
            pltpu.VMEM((own, kept), f32),
            pltpu.VMEM((steps, train), f32),
            pltpu.VMEM((steps, own, kept), f32),
            pltpu.VMEM((d_in, train), bf16),
            pltpu.VMEM((share, train), bf16),
            pltpu.VMEM((kept, own), bf16),
            pltpu.VMEM((steps - 1, share, train), f32),
            pltpu.VMEM((steps - 1, kept, own), f32),
            pltpu.VMEM((2, kept, own), bf16),
            pltpu.VMEM((2, share, train), bf16),
            pltpu.VMEM((paths, 256), f32),
            pltpu.VMEM((parts, kept, window // parts), bf16),
            pltpu.VMEM((parts, kept, window // parts), bf16),
            dma((steps, n, 7)), dma((steps, n, 7)), dma((steps, n, 8)), dma((steps, n, 8)),
            dma((steps, rows // 2)), dma((steps, rows // 2)),
            dma((2, rows // 2)), dma((2, rows // 2)),
            dma((3 + parts,)), dma((3 + parts,)),
        ],
        compiler_params=pltpu.CompilerParams(
            collective_id=0, has_side_effects=True, vmem_limit_bytes=44 * 1024 * 1024
        ),
    )(
        *(pltpu.with_memory_space_constraint(a, pltpu.HBM) for a in (
            x_train, targets[None, :], noise_draws.T, alpha_init.T, velocity_init.T, frequencies,
            phases[None, :], path_weights, x_window, batch_index,
        ))
    )
    return alpha.T, velocity.T, prior


def fits(mesh, args):
    x_train, batch_index, path_weights, x_window = args[0], args[9], args[7], args[8]
    rows = mesh.shape["row"]
    d_in, train = x_train.shape
    feat, paths = path_weights.shape
    return (
        mesh.shape["col"] == 2 and rows == 16 and d_in == 64 and train == 256 * rows
        and paths == 16 * rows and feat % 1024 == 0 and x_window.shape[1] == 2048
        and batch_index.shape[0] == 3 and batch_index.shape[1] % (256 * rows) == 0
    )


def solution(mesh):
    def body(*args):
        return (fused_shards if fits(mesh, args) else shards)(*args)

    placed = (
        P(None, "col"),
        P("col"),
        P("col", "row"),
        P("col", "row"),
        P("col", "row"),
        P(None, "col"),
        P("col"),
        P("col", None),
        P(None, "row"),
        P(),
    )
    return jax.shard_map(
        body,
        mesh=mesh,
        in_specs=placed,
        out_specs=(P("col", "row"), P("col", "row"), P("col", "row")),
        check_vma=False,
    )
```

time: 116 us -> 76.2 us (0.66)
  Pallas kernels: 111 us -> 73 us
  local copies, waits for them, and re-layouts: 4.03 us -> 2.38 us
    pallas_call x1, Pallas kernels: 111 us -> 73 us  [fused_shards(): pl.pallas_call(functools.partial(fused_kernel, coeffs, steps, rows, PIECE...]
    unnamed x22 -> x3, local copies, waits for them, and re-layouts: 4.03 us -> 2.38 us
where the time goes in v1:
time: 76.2 us; the launch traced here: 76.1 us
  Pallas kernels  73 us (96%)
  local copies, waits for them, and re-layouts  2.38 us (3%)
    pallas_call x1, Pallas kernels, fused_shards(): pl.pallas_call(functools.partial(fused_kernel, coeffs, steps, rows, PIECE...  73 us
    unnamed x3, local copies, waits for them, and re-layouts  2.38 us

profile of v1, /device:TPU:0, one launch (start us, length us, event | category | flops | bytes accessed | tf_op | source)
XLA Modules:
  0.0 76.1 jit_solution(6780404329252023352)
XLA Ops:
  0.6 73.0 %shard_map.121 = (f32[16,4096]{1,0:T(8,128)S(1)}, f32[16,4096]{1,0:T(8,128)S(1)}, f32[128,2048]{1,0:T(8,128)S(1)}) custom-call(bf16[64,4096]{1,0:T(8,128)(2,1)} %x_hbm.1, f32[1,4096]{1,0:T(1,128)} %bitcast.12, f32[16,4096]{1,0:T(8,128)} %bitcast.9, f32[16,4096]{1,0:T(8,128)} %bitcast.10, f32[16,4096]{1,0:T(8,128)} %bitcast.11, bf16[64,2048]{1,0:T(8,128)(2,1)} %freq_hbm.1, ...), custom_call_target="tpu_custom_call" | custom-call | tf_op jit(solution)/shard_map/pallas_call | solution.py:656
  73.7 0.7 copy.16
  74.4 0.7 copy.17
  75.1 1.0 %copy.18 = f32[128,2048]{1,0:T(8,128)} copy(f32[128,2048]{1,0:T(8,128)S(1)} %get-tuple-element.14) | data formatting | bytes 2097152

commit v2 on v1

--- a/solution.py
+++ b/solution.py
@@ -169,7 +169,7 @@
 LOADS = (
     "alpha", "x", "index", "target", "noise", "velocity", "freq", "phase", "weight", "window",
 )
-PIECES = ((0, 256, "yxz"), (256, 256, "yzx"))
+PIECES = ((0, 128, "yxz"), (128, 128, "yzx"), (256, 128, "yxz"), (384, 128, "yzx"))
 MASKS = ("y", "x", "z", "yx", "yz", "xz", "yxz")
 
 
@@ -184,9 +184,9 @@
     window_ref, index_ref, load_sem,
     gathered, tile, train_aug, window_aug, point_aug, freq_t, weight_t, phi_buf, acc,
     pull_a, pull_v, prior_t, prior_out, prior_in, count_ref, count_t, x_in, start_out, start_in, entry_out, entry_in,
-    exit_out, exit_in, window_acc, window_out, window_in,
+    exit_out, exit_in, window_out, window_in,
     hop_send, hop_recv, pair_send, pair_recv, entry_send, entry_recv, exit_send, exit_recv,
-    misc_send, misc_recv,
+    misc_send, misc_recv, x_send, x_recv,
 ):
     div, rem = lax.div, lax.rem
     f32, bf16 = jnp.float32, jnp.bfloat16
@@ -294,14 +294,22 @@
         for q in count:
             pair(step, "", q).start()
 
-    def relay(step, which):
+    def relay(step, which, ahead=None):
         for q in count:
             order = pieces[q][2]
             mask = mask_of([order[i] for i in which])
             arrival(step, mask, q).wait_recv()
-            for d in order[max(which) + 1 :]:
+            for d in order[max(which) + 1 : ahead]:
                 hop(step, mask, d, q).start()
             pair(step, mask, q).start()
+
+    def relay_first(step):
+        relay(step, (0,), 2)
+        for q in count:
+            order = pieces[q][2]
+            hop(step, order[0], order[2], q).start()
+        relay(step, (1,))
+        relay(step, (2,))
 
     def product(step, masks):
         for mask in masks:
@@ -313,22 +321,20 @@
         span = at(first, wide * own)
         return dot(tile[:, span], gathered[step, span, :])
 
-    def x_copy():
-        half = train // 2
-        cols = at(core * half, half)
+    def x_span(on_core, part):
+        width = train // 4
+        return at((on_core * 2 + part) * width, width)
+
+    def x_copy(part):
+        cols = x_span(core, part)
         return remote(
-            x_ref.at[:, cols], x_in.at[:, cols], misc_send.at[0], misc_recv.at[0], (row, peer)
-        )
-
-    def x_pair():
-        half = train // 2
-        ref = x_in.at[:, at(core * half, half)]
-        return remote(ref, ref, misc_send.at[1], misc_recv.at[1], (sibling, col))
-
-    def x_twin():
-        half = train // 2
-        ref = x_in.at[:, at((1 - core) * half, half)]
-        return remote(ref, ref, misc_send.at[1], misc_recv.at[1], (sibling, col))
+            x_ref.at[:, cols], x_in.at[:, cols], x_send.at[0, part], x_recv.at[0, part],
+            (row, peer),
+        )
+
+    def x_pair(part, twin=False):
+        ref = x_in.at[:, x_span(1 - core if twin else core, part)]
+        return remote(ref, ref, x_send.at[1, part], x_recv.at[1, part], (sibling, col))
 
     def prior_copy():
         return remote(prior_out, prior_in, misc_send.at[2], misc_recv.at[2], (row, peer))
@@ -458,104 +464,91 @@
         for i in range(train // lanes):
             count_ref[step : step + 1, i * lanes : (i + 1) * lanes] = table[i : i + 1, :]
 
-    def spread_counts():
-        for step in range(steps):
-            line = count_ref[step : step + 1, at(local * own, own)]
-            count_t[step] = jnp.broadcast_to(line, (kept, own)).T
-
-    def fill_phi(rhs, first, n):
-        width = 512
-
-        def one(i):
-            turns = dot(freq_t[at(first + i * width, width), :], rhs)
-            phi_buf[at(i * width, width), :] = scaled_cos(turns, scale_coeffs).astype(bf16)
-
-        loop(n // width, one)
+    def spread_counts(step):
+        line = count_ref[step : step + 1, at(local * own, own)]
+        count_t[step] = jnp.broadcast_to(line, (kept, own)).T
+
+    def sums_over_features(rhs, weights):
+        phi_buf[...] = scaled_cos(dot(freq_t[...], rhs), scale_coeffs).astype(bf16)
+        return dot(weights, phi_buf[...])
 
     def prior_points(c, out):
-        def one(i):
-            fill_phi(train_aug[:, at(c * train + local * own + i * block, block)], 0, feat)
-            out[at(i * block, block), :] = dot(weight_t[at(group * kept, kept), :], phi_buf[...]).T
-
-        loop(own // block, one)
+        rhs = train_aug[:, at(c * train + local * own, own)]
+        out[...] = sums_over_features(rhs, weight_t[at(group * kept, kept), :]).T
 
     def fill_tile(i):
-        cols = at(i * block, block)
-        dist_sq = jnp.maximum(dot(point_aug[...], train_aug[:, cols]), 1e-30)
-        scaled = dist_sq * lax.rsqrt(dist_sq)
-        tile[:, cols] = ((1.0 + scaled) * jnp.exp(-scaled)).astype(bf16)
-
-    tiles = train // block
+        for part in range(2):
+            cols = at(i * 4 * block + part * 2 * block, 2 * block)
+            for half in range(2):
+                span = slice(half * own // 2, (half + 1) * own // 2)
+                dist_sq = jnp.maximum(dot(point_aug[span, :], train_aug[:, cols]), 1e-30)
+                scaled = dist_sq * lax.rsqrt(dist_sq)
+                tile[span, cols] = ((1.0 + scaled) * jnp.exp(-scaled)).astype(bf16)
+
+    tiles = train // (4 * block)
 
     def fill_tiles(c, first, n):
         loop(n, lambda i: fill_tile(c * tiles + first + i))
 
-    def window_work(i, f):
-        half = feat // 2
-        span = at(i * block, block)
-        fill_phi(window_aug[:, span], f * half, half)
-        sums = dot(weight_t[:, at(f * half, half)], phi_buf[:half, :])
-        if f == 0:
-            window_acc[...] = sums
-            return
-        total = window_acc[...] + sums
+    def window_work(i):
+        width = window // parts
+        span = slice(i * width, (i + 1) * width)
+        total = sums_over_features(window_aug[:, span], weight_t[...])
         prior_ref[:, span] = jnp.where(col == 0, total[:kept], total[kept:])
-        per = window // block // parts
-        window_out[i // per, :, (i % per) * block : (i % per + 1) * block] = jnp.where(
-            col == 0, total[kept:], total[:kept]
-        ).astype(bf16)
-        if i % per == per - 1:
-            window_copy(i // per).start()
+        window_out[i] = jnp.where(col == 0, total[kept:], total[:kept]).astype(bf16)
+        window_copy(i).start()
 
     loaded("alpha")
     start_out[...] = alpha_in[...].astype(bf16)
     pl.semaphore_wait(barrier, team)
     send_entry(0, None)
     loaded("x")
-    x_copy().start()
-    loaded("index")
-    for step in range(steps):
-        count_points(step)
-    loaded("target", "noise", "velocity")
-    base = noise_ref[...] - target_ref[...]
-    speed = velocity_in[...]
-    free = alpha_in[...]
-    for step in range(steps):
-        speed = MOMENTUM * speed - STEP_SIZE * (
-            count_ref[step : step + 1, :] * (NOISE_VAR * free + base)
-        )
-        if step < steps - 1:
-            free = free + speed
-            send_entry(1 + step, free)
-    alpha_ref[...] = free
-    velocity_ref[...] = speed
+    x_copy(0).start()
     add_train(x_ref, col)
     add_points()
-    fill_tiles(col, 0, 4)
+    fill_tiles(col, 0, 1)
+    loaded("index")
+    count_points(0)
     gathered[0, at(first_row(row, col), own), :] = take_entry(0).astype(bf16)
     start_gather(0)
+    x_copy(1).start()
     loaded("freq", "phase", "weight")
     add_freq()
-    fill_tiles(col, 4, tiles - 4)
-    relay(0, (0,))
-    relay(0, (1,))
-    relay(0, (2,))
-    x_copy().wait_recv()
-    x_pair().start()
+    fill_tiles(col, 1, tiles - 1)
+    count_points(1)
+    relay_first(0)
+    x_copy(0).wait_recv()
+    x_pair(0).start()
     prior_points(col, prior_t)
+    x_copy(1).wait_recv()
+    x_pair(1).start()
+    for step in range(steps - 1):
+        spread_counts(step)
+    loaded("window")
+    add_window()
     relay(0, (0, 1))
-    x_twin().wait_recv()
+    for part in (0, 1):
+        x_pair(part, True).wait_recv()
     add_train(x_in, peer)
     prior_points(peer, prior_out)
     prior_copy().start()
     relay(0, (0, 2))
     relay(0, (1, 2))
+    loaded("target", "noise", "velocity")
+    base = noise_ref[...] - target_ref[...]
+    speed = velocity_in[...]
+    free = alpha_in[...]
+    for step in range(steps - 1):
+        speed = MOMENTUM * speed - STEP_SIZE * (
+            count_ref[step : step + 1, :] * (NOISE_VAR * free + base)
+        )
+        free = free + speed
+        send_entry(1 + step, free)
+    alpha_ref[...] = free
+    velocity_ref[...] = speed
     fill_tiles(peer, 0, tiles // 2)
     relay(0, (0, 1, 2))
     fill_tiles(peer, tiles // 2, tiles // 2)
-    spread_counts()
-    loaded("window")
-    add_window()
     for mask in ("",) + MASKS:
         for q in count:
             pair(0, mask, q, True).wait_recv()
@@ -581,29 +574,27 @@
         pull_a[...] = pull
         gathered[step, at(first_row(row, col), own), :] = (take_entry(step) + pull).astype(bf16)
         start_gather(step)
-        chunks = window // block // (steps - 1)
-        work = [
-            (lambda i, f: lambda: window_work(i, f))((step - 1) * chunks + i, f)
-            for i in range(chunks) for f in (0, 1)
-        ]
-
-        def run(n):
-            for _ in range(n):
-                work.pop(0)()
-
-        run(3)
-        relay(step, (0,))
-        relay(step, (1,))
-        relay(step, (2,))
-        run(2)
+        chunks = parts // (steps - 1)
+        first = (step - 1) * chunks
+        window_work(first)
+        relay_first(step)
+        acc[...] = product(step, ("", "x"))
+        if step == 1:
+            count_points(steps - 1)
+            spread_counts(steps - 1)
         relay(step, (0, 1))
-        acc[...] = product(step, ("", "x"))
-        run(1)
+        for i in range(1, chunks):
+            window_work(first + i)
+        if step == 1:
+            final = count_ref[steps - 1 : steps, :]
+            base = noise_ref[...] - target_ref[...]
+            velocity_ref[...] = MOMENTUM * velocity_ref[...] - STEP_SIZE * (
+                final * (NOISE_VAR * alpha_ref[...] + base)
+            )
         relay(step, (0, 2))
         relay(step, (1, 2))
         if step == steps - 1:
             send_exit(0, pull_a[...])
-        run(len(work))
         acc[...] += product(step, ("y", "yx"))
         relay(step, (0, 1, 2))
         acc[...] += product(step, ("z", "xz"))
@@ -619,8 +610,9 @@
     speed = velocity_ref[...] + take_exit(1)
     velocity_ref[...] = speed
     alpha_ref[...] += speed
-    x_copy().wait_send()
-    x_pair().wait_send()
+    for part in (0, 1):
+        x_copy(part).wait_send()
+        x_pair(part).wait_send()
     prior_copy().wait_send()
     for kind in range(steps):
         loop(team - 1, lambda d: entry_copy(kind, d).wait_send())
@@ -681,7 +673,7 @@
             pltpu.VMEM((own, 4 * d_in), bf16),
             pltpu.VMEM((feat, 4 * d_in), bf16),
             pltpu.VMEM((paths, feat), bf16),
-            pltpu.VMEM((feat, 256), bf16),
+            pltpu.VMEM((feat, own), bf16),
             pltpu.VMEM((own, kept), f32),
             pltpu.VMEM((own, kept), f32),
             pltpu.VMEM((own, kept), f32),
@@ -697,13 +689,12 @@
             pltpu.VMEM((steps - 1, kept, own), f32),
             pltpu.VMEM((2, kept, own), bf16),
             pltpu.VMEM((2, share, train), bf16),
-            pltpu.VMEM((paths, 256), f32),
             pltpu.VMEM((parts, kept, window // parts), bf16),
             pltpu.VMEM((parts, kept, window // parts), bf16),
             dma((steps, n, 7)), dma((steps, n, 7)), dma((steps, n, 8)), dma((steps, n, 8)),
             dma((steps, rows // 2)), dma((steps, rows // 2)),
             dma((2, rows // 2)), dma((2, rows // 2)),
-            dma((3 + parts,)), dma((3 + parts,)),
+            dma((3 + parts,)), dma((3 + parts,)), dma((2, 2)), dma((2, 2)),
         ],
         compiler_params=pltpu.CompilerParams(
             collective_id=0, has_side_effects=True, vmem_limit_bytes=44 * 1024 * 1024

time: 76.2 us -> 68 us (0.89)
  Pallas kernels: 73 us -> 64.8 us
    pallas_call x1, Pallas kernels: 73 us -> 64.8 us  [fused_shards(): pl.pallas_call(functools.partial(fused_kernel, coeffs, steps, rows, PIECE...]
where the time goes in v2:
time: 68 us; the launch traced here: 67.9 us
  Pallas kernels  64.8 us (95%)
  local copies, waits for them, and re-layouts  2.38 us (4%)
    pallas_call x1, Pallas kernels, fused_shards(): pl.pallas_call(functools.partial(fused_kernel, coeffs, steps, rows, PIECE...  64.8 us
    unnamed x3, local copies, waits for them, and re-layouts  2.38 us

profile of v2, /device:TPU:0, one launch (start us, length us, event | category | flops | bytes accessed | tf_op | source)
XLA Modules:
  0.0 67.9 jit_solution(1787917819052292659)
XLA Ops:
  0.6 64.8 %shard_map.121 = (f32[16,4096]{1,0:T(8,128)S(1)}, f32[16,4096]{1,0:T(8,128)S(1)}, f32[128,2048]{1,0:T(8,128)S(1)}) custom-call(bf16[64,4096]{1,0:T(8,128)(2,1)} %x_hbm.1, f32[1,4096]{1,0:T(1,128)} %bitcast.12, f32[16,4096]{1,0:T(8,128)} %bitcast.9, f32[16,4096]{1,0:T(8,128)} %bitcast.10, f32[16,4096]{1,0:T(8,128)} %bitcast.11, bf16[64,2048]{1,0:T(8,128)(2,1)} %freq_hbm.1, ...), custom_call_target="tpu_custom_call" | custom-call | tf_op jit(solution)/shard_map/pallas_call | solution.py:648
  65.5 0.7 %copy.16 = f32[4096,16]{0,1:T(8,128)} copy(f32[4096,16]{0,1:T(8,128)S(1)} %bitcast.8) | data formatting | bytes 524288
  66.2 0.7 %copy.17 = f32[4096,16]{0,1:T(8,128)} copy(f32[4096,16]{0,1:T(8,128)S(1)} %bitcast.7) | data formatting | bytes 524288
  66.9 1.0 %copy.18 = f32[128,2048]{1,0:T(8,128)} copy(f32[128,2048]{1,0:T(8,128)S(1)} %get-tuple-element.14) | data formatting | bytes 2097152

commit v3 on v2

--- a/solution.py
+++ b/solution.py
@@ -186,7 +186,7 @@
     pull_a, pull_v, prior_t, prior_out, prior_in, count_ref, count_t, x_in, start_out, start_in, entry_out, entry_in,
     exit_out, exit_in, window_out, window_in,
     hop_send, hop_recv, pair_send, pair_recv, entry_send, entry_recv, exit_send, exit_recv,
-    misc_send, misc_recv, x_send, x_recv,
+    misc_send, misc_recv, x_send, x_recv, free_t, point_in, mate_aug,
 ):
     div, rem = lax.div, lax.rem
     f32, bf16 = jnp.float32, jnp.bfloat16
@@ -294,22 +294,18 @@
         for q in count:
             pair(step, "", q).start()
 
-    def relay(step, which, ahead=None):
+    def relay(step, which):
         for q in count:
             order = pieces[q][2]
             mask = mask_of([order[i] for i in which])
             arrival(step, mask, q).wait_recv()
-            for d in order[max(which) + 1 : ahead]:
+            for d in order[max(which) + 1 :]:
                 hop(step, mask, d, q).start()
             pair(step, mask, q).start()
 
     def relay_first(step):
-        relay(step, (0,), 2)
-        for q in count:
-            order = pieces[q][2]
-            hop(step, order[0], order[2], q).start()
-        relay(step, (1,))
-        relay(step, (2,))
+        for stage in range(3):
+            relay(step, (stage,))
 
     def product(step, masks):
         for mask in masks:
@@ -335,6 +331,12 @@
     def x_pair(part, twin=False):
         ref = x_in.at[:, x_span(1 - core if twin else core, part)]
         return remote(ref, ref, x_send.at[1, part], x_recv.at[1, part], (sibling, col))
+
+    def point_copy():
+        return remote(
+            x_ref.at[:, at(local * own, own)], point_in, x_send.at[2, 0], x_recv.at[2, 0],
+            (row, peer),
+        )
 
     def prior_copy():
         return remote(prior_out, prior_in, misc_send.at[2], misc_recv.at[2], (row, peer))
@@ -472,8 +474,12 @@
         phi_buf[...] = scaled_cos(dot(freq_t[...], rhs), scale_coeffs).astype(bf16)
         return dot(weights, phi_buf[...])
 
-    def prior_points(c, out):
-        rhs = train_aug[:, at(c * train + local * own, own)]
+    def add_mate():
+        for part in range(3):
+            mate_aug[part * d_in : (part + 1) * d_in, :] = point_in[...]
+        mate_aug[3 * d_in :, :] = tail_rows([1.0] * 3, d_in, own).astype(bf16)
+
+    def prior_points(rhs, out):
         out[...] = sums_over_features(rhs, weight_t[at(group * kept, kept), :]).T
 
     def fill_tile(i):
@@ -500,55 +506,62 @@
 
     loaded("alpha")
     start_out[...] = alpha_in[...].astype(bf16)
+    loaded("x")
+    add_points()
     pl.semaphore_wait(barrier, team)
     send_entry(0, None)
-    loaded("x")
+    point_copy().start()
     x_copy(0).start()
     add_train(x_ref, col)
-    add_points()
     fill_tiles(col, 0, 1)
     loaded("index")
     count_points(0)
+    count_points(1)
     gathered[0, at(first_row(row, col), own), :] = take_entry(0).astype(bf16)
     start_gather(0)
     x_copy(1).start()
     loaded("freq", "phase", "weight")
     add_freq()
+    point_copy().wait_recv()
+    add_mate()
+    prior_points(mate_aug[...], prior_out)
+    prior_copy().start()
     fill_tiles(col, 1, tiles - 1)
-    count_points(1)
     relay_first(0)
+    prior_points(train_aug[:, at(col * train + local * own, own)], prior_t)
     x_copy(0).wait_recv()
     x_pair(0).start()
-    prior_points(col, prior_t)
-    x_copy(1).wait_recv()
-    x_pair(1).start()
     for step in range(steps - 1):
         spread_counts(step)
     loaded("window")
     add_window()
-    relay(0, (0, 1))
-    for part in (0, 1):
-        x_pair(part, True).wait_recv()
-    add_train(x_in, peer)
-    prior_points(peer, prior_out)
-    prior_copy().start()
-    relay(0, (0, 2))
-    relay(0, (1, 2))
+    x_copy(1).wait_recv()
+    x_pair(1).start()
     loaded("target", "noise", "velocity")
     base = noise_ref[...] - target_ref[...]
     speed = velocity_in[...]
     free = alpha_in[...]
+    frees = []
     for step in range(steps - 1):
         speed = MOMENTUM * speed - STEP_SIZE * (
             count_ref[step : step + 1, :] * (NOISE_VAR * free + base)
         )
         free = free + speed
-        send_entry(1 + step, free)
+        frees.append(free)
     alpha_ref[...] = free
     velocity_ref[...] = speed
-    fill_tiles(peer, 0, tiles // 2)
+    for part in (0, 1):
+        x_pair(part, True).wait_recv()
+    add_train(x_in, peer)
+    fill_tiles(peer, 0, 1)
+    relay(0, (0, 1))
+    send_entry(1, frees[0])
+    fill_tiles(peer, 1, 1)
+    relay(0, (0, 2))
+    relay(0, (1, 2))
+    send_entry(2, frees[1])
+    fill_tiles(peer, 2, tiles - 2)
     relay(0, (0, 1, 2))
-    fill_tiles(peer, tiles // 2, tiles // 2)
     for mask in ("",) + MASKS:
         for q in count:
             pair(0, mask, q, True).wait_recv()
@@ -572,31 +585,34 @@
             break
         pull_v[...] = speed
         pull_a[...] = pull
-        gathered[step, at(first_row(row, col), own), :] = (take_entry(step) + pull).astype(bf16)
+        free = take_entry(1) if step == 1 else free_t[...]
+        gathered[step, at(first_row(row, col), own), :] = (free + pull).astype(bf16)
         start_gather(step)
         chunks = parts // (steps - 1)
         first = (step - 1) * chunks
         window_work(first)
         relay_first(step)
-        acc[...] = product(step, ("", "x"))
+        for i in range(1, chunks):
+            window_work(first + i)
+        relay(step, (0, 1))
+        acc[...] = product(step, ("",))
         if step == 1:
             count_points(steps - 1)
             spread_counts(steps - 1)
-        relay(step, (0, 1))
-        for i in range(1, chunks):
-            window_work(first + i)
+        acc[...] += product(step, ("x",))
+        relay(step, (0, 2))
+        relay(step, (1, 2))
+        if step == steps - 1:
+            send_exit(0, pull_a[...])
+        acc[...] += product(step, ("y", "yx"))
+        relay(step, (0, 1, 2))
         if step == 1:
             final = count_ref[steps - 1 : steps, :]
             base = noise_ref[...] - target_ref[...]
             velocity_ref[...] = MOMENTUM * velocity_ref[...] - STEP_SIZE * (
                 final * (NOISE_VAR * alpha_ref[...] + base)
             )
-        relay(step, (0, 2))
-        relay(step, (1, 2))
-        if step == steps - 1:
-            send_exit(0, pull_a[...])
-        acc[...] += product(step, ("y", "yx"))
-        relay(step, (0, 1, 2))
+            free_t[...] = take_entry(2)
         acc[...] += product(step, ("z", "xz"))
         acc[...] += product(step, ("yz",))
         acc[...] += product(step, ("yxz",))
@@ -614,6 +630,7 @@
         x_copy(part).wait_send()
         x_pair(part).wait_send()
     prior_copy().wait_send()
+    point_copy().wait_send()
     for kind in range(steps):
         loop(team - 1, lambda d: entry_copy(kind, d).wait_send())
     for kind in range(2):
@@ -694,7 +711,10 @@
             dma((steps, n, 7)), dma((steps, n, 7)), dma((steps, n, 8)), dma((steps, n, 8)),
             dma((steps, rows // 2)), dma((steps, rows // 2)),
             dma((2, rows // 2)), dma((2, rows // 2)),
-            dma((3 + parts,)), dma((3 + parts,)), dma((2, 2)), dma((2, 2)),
+            dma((3 + parts,)), dma((3 + parts,)), dma((3, 2)), dma((3, 2)),
+            pltpu.VMEM((own, kept), f32),
+            pltpu.VMEM((d_in, own), bf16),
+            pltpu.VMEM((4 * d_in, own), bf16),
         ],
         compiler_params=pltpu.CompilerParams(
             collective_id=0, has_side_effects=True, vmem_limit_bytes=44 * 1024 * 1024

time: 68 us -> 66 us (0.971)
  Pallas kernels: 64.8 us -> 62.8 us
    pallas_call x1, Pallas kernels: 64.8 us -> 62.8 us  [fused_shards(): pl.pallas_call(functools.partial(fused_kernel, coeffs, steps, rows, PIECE...]
where the time goes in v3:
time: 66 us; the launch traced here: 65.9 us
  Pallas kernels  62.8 us (95%)
  local copies, waits for them, and re-layouts  2.38 us (4%)
    pallas_call x1, Pallas kernels, fused_shards(): pl.pallas_call(functools.partial(fused_kernel, coeffs, steps, rows, PIECE...  62.8 us
    unnamed x3, local copies, waits for them, and re-layouts  2.38 us

profile of v3, /device:TPU:0, one launch (start us, length us, event | category | flops | bytes accessed | tf_op | source)
XLA Modules:
  0.0 65.9 jit_solution(12222800218669241499)
XLA Ops:
  0.6 62.8 %shard_map.121 = (f32[16,4096]{1,0:T(8,128)S(1)}, f32[16,4096]{1,0:T(8,128)S(1)}, f32[128,2048]{1,0:T(8,128)S(1)}) custom-call(bf16[64,4096]{1,0:T(8,128)(2,1)} %x_hbm.1, f32[1,4096]{1,0:T(1,128)} %bitcast.12, f32[16,4096]{1,0:T(8,128)} %bitcast.9, f32[16,4096]{1,0:T(8,128)} %bitcast.10, f32[16,4096]{1,0:T(8,128)} %bitcast.11, bf16[64,2048]{1,0:T(8,128)(2,1)} %freq_hbm.1, ...), custom_call_target="tpu_custom_call" | custom-call | tf_op jit(solution)/shard_map/pallas_call | solution.py:665
  63.5 0.7 %copy.16 = f32[4096,16]{0,1:T(8,128)} copy(f32[4096,16]{0,1:T(8,128)S(1)} %bitcast.8) | data formatting | bytes 524288
  64.2 0.7 %copy.17 = f32[4096,16]{0,1:T(8,128)} copy(f32[4096,16]{0,1:T(8,128)S(1)} %bitcast.7) | data formatting | bytes 524288
  64.9 1.0 %copy.18 = f32[128,2048]{1,0:T(8,128)} copy(f32[128,2048]{1,0:T(8,128)S(1)} %get-tuple-element.14) | data formatting | bytes 2097152

commit v4 on v3

--- a/solution.py
+++ b/solution.py
@@ -169,7 +169,7 @@
 LOADS = (
     "alpha", "x", "index", "target", "noise", "velocity", "freq", "phase", "weight", "window",
 )
-PIECES = ((0, 128, "yxz"), (128, 128, "yzx"), (256, 128, "yxz"), (384, 128, "yzx"))
+ORDERS = ("yxz", "yzx", "yxz", "yzx")
 MASKS = ("y", "x", "z", "yx", "yz", "xz", "yxz")
 
 
@@ -528,6 +528,20 @@
     prior_copy().start()
     fill_tiles(col, 1, tiles - 1)
     relay_first(0)
+    loaded("target", "noise", "velocity")
+    base = noise_ref[...] - target_ref[...]
+    speed = velocity_in[...]
+    free = alpha_in[...]
+    frees = []
+    for step in range(steps - 1):
+        speed = MOMENTUM * speed - STEP_SIZE * (
+            count_ref[step : step + 1, :] * (NOISE_VAR * free + base)
+        )
+        free = free + speed
+        frees.append(free)
+    alpha_ref[...] = free
+    velocity_ref[...] = speed
+    send_entry(1, frees[0])
     prior_points(train_aug[:, at(col * train + local * own, own)], prior_t)
     x_copy(0).wait_recv()
     x_pair(0).start()
@@ -537,25 +551,11 @@
     add_window()
     x_copy(1).wait_recv()
     x_pair(1).start()
-    loaded("target", "noise", "velocity")
-    base = noise_ref[...] - target_ref[...]
-    speed = velocity_in[...]
-    free = alpha_in[...]
-    frees = []
-    for step in range(steps - 1):
-        speed = MOMENTUM * speed - STEP_SIZE * (
-            count_ref[step : step + 1, :] * (NOISE_VAR * free + base)
-        )
-        free = free + speed
-        frees.append(free)
-    alpha_ref[...] = free
-    velocity_ref[...] = speed
     for part in (0, 1):
         x_pair(part, True).wait_recv()
     add_train(x_in, peer)
     fill_tiles(peer, 0, 1)
     relay(0, (0, 1))
-    send_entry(1, frees[0])
     fill_tiles(peer, 1, 1)
     relay(0, (0, 2))
     relay(0, (1, 2))
@@ -661,9 +661,10 @@
     vmem = pl.BlockSpec(memory_space=pltpu.VMEM)
     dma = pltpu.SemaphoreType.DMA
     f32, bf16 = jnp.float32, jnp.bfloat16
-    n = len(PIECES)
+    n = len(ORDERS)
+    pieces = tuple((i * (own // n), own // n, order) for i, order in enumerate(ORDERS))
     alpha, velocity, prior = pl.pallas_call(
-        functools.partial(fused_kernel, coeffs, steps, rows, PIECES),
+        functools.partial(fused_kernel, coeffs, steps, rows, pieces),
         in_specs=[pl.BlockSpec(memory_space=pltpu.HBM)] * 10,
         out_specs=[vmem] * 3,
         out_shape=(
@@ -730,13 +731,15 @@
 
 def fits(mesh, args):
     x_train, batch_index, path_weights, x_window = args[0], args[9], args[7], args[8]
-    rows = mesh.shape["row"]
+    rows, cols = mesh.shape["row"], mesh.shape["col"]
     d_in, train = x_train.shape
     feat, paths = path_weights.shape
+    steps, batch = batch_index.shape
+    own = 2 * train // rows
     return (
-        mesh.shape["col"] == 2 and rows == 16 and d_in == 64 and train == 256 * rows
-        and paths == 16 * rows and feat % 1024 == 0 and x_window.shape[1] == 2048
-        and batch_index.shape[0] == 3 and batch_index.shape[1] % (256 * rows) == 0
+        (rows, cols, steps) == (16, 2, 3) and d_in % 32 == 0 and train % 1024 == 0
+        and own % 512 == 0 and paths % (16 * rows) == 0 and feat % 256 == 0
+        and x_window.shape[1] == 4 * own and batch % (128 * rows * cols) == 0
     )
 
 

time: 66 us -> 68.4 us (1.036)
  Pallas kernels: 62.8 us -> 65.3 us
    pallas_call x1, Pallas kernels: 62.8 us -> 65.3 us  [fused_shards(): pl.pallas_call(functools.partial(fused_kernel, coeffs, steps, rows, piece...]
where the time goes in v4:
time: 68.4 us; the launch traced here: 68.3 us
  Pallas kernels  65.3 us (95%)
  local copies, waits for them, and re-layouts  2.38 us (3%)
    pallas_call x1, Pallas kernels, fused_shards(): pl.pallas_call(functools.partial(fused_kernel, coeffs, steps, rows, piece...  65.3 us
    unnamed x3, local copies, waits for them, and re-layouts  2.38 us

profile of v4, /device:TPU:0, one launch (start us, length us, event | category | flops | bytes accessed | tf_op | source)
XLA Modules:
  0.0 68.3 jit_solution(15956246609278065809)
XLA Ops:
  0.6 65.3 %shard_map.121 = (f32[16,4096]{1,0:T(8,128)S(1)}, f32[16,4096]{1,0:T(8,128)S(1)}, f32[128,2048]{1,0:T(8,128)S(1)}) custom-call(bf16[64,4096]{1,0:T(8,128)(2,1)} %x_hbm.1, f32[1,4096]{1,0:T(1,128)} %bitcast.12, f32[16,4096]{1,0:T(8,128)} %bitcast.9, f32[16,4096]{1,0:T(8,128)} %bitcast.10, f32[16,4096]{1,0:T(8,128)} %bitcast.11, bf16[64,2048]{1,0:T(8,128)(2,1)} %freq_hbm.1, ...), custom_call_target="tpu_custom_call" | custom-call | tf_op jit(solution)/shard_map/pallas_call | solution.py:666
  65.9 0.7 %copy.16 = f32[4096,16]{0,1:T(8,128)} copy(f32[4096,16]{0,1:T(8,128)S(1)} %bitcast.8) | data formatting | bytes 524288
  66.6 0.7 %copy.17 = f32[4096,16]{0,1:T(8,128)} copy(f32[4096,16]{0,1:T(8,128)S(1)} %bitcast.7) | data formatting | bytes 524288
  67.3 1.0 %copy.18 = f32[128,2048]{1,0:T(8,128)} copy(f32[128,2048]{1,0:T(8,128)S(1)} %get-tuple-element.14) | data formatting | bytes 2097152
